TPU v7x, 128 devices: a whole 4x4x4 slice. The times are simulated.
128 devices in a mesh: gx: 8 (over z_lo, x), gy: 4 (over z_hi, core), gz: 4 (over y).
Axes of the slice: x: 4, y: 4, z: 4 (z_hi: 2, z_lo: 2; z = z_hi * 2 + z_lo), core: 2. Of those that a mesh axis runs over, the one named last changes fastest.
Arguments:
- x_saved: bfloat16 [1024, 16384], P('gx', ('gy', 'gz')), may hold values from -0.1875 to 0.1875
- grad_out: bfloat16 [1024, 28672], P('gx', ('gz', 'gy')), may hold values from -6 to 6
- weight: bfloat16 [16384, 28672], P('gy', ('gz', 'gx')), may hold values from -0.09375 to 0.09375
Outputs:
- grad_in: bfloat16 [1024, 16384], P('gx', ('gy', 'gz'))
- grad_weight: bfloat16 [16384, 28672], P('gy', ('gz', 'gx'))
All inputs are finite; a program needn't handle non-finite values.
Results may differ from a plain program's by a relative error of at most 0.001.
Values may be sent and summed in bfloat16 or wider, within the bound.
A program may use at most 128 MiB of HBM per device.

v0:
```python
import jax
import jax.numpy as jnp
from jax import lax
from jax.sharding import PartitionSpec as P


def body(x_saved, grad_out, weight):
    token_rows = x_saved.shape[0]
    token_groups = lax.axis_size("gx")
    feature_groups = lax.axis_size("gz")
    grad_block = lax.all_gather(grad_out, "gy", axis=1, tiled=True)
    grad_all = lax.all_to_all(grad_block, "gx", split_axis=1, concat_axis=0, tiled=True)
    unit_cols = grad_all.shape[1]
    inputs_block = lax.all_gather(x_saved, "gz", axis=1, tiled=True)
    summed = jnp.einsum(
        "td,tc->dc",
        lax.all_gather(inputs_block, "gx", axis=0, tiled=True),
        grad_all,
        preferred_element_type=jnp.float32,
    )
    grad_weight = summed.astype(jnp.bfloat16)
    grad_split = grad_all.reshape(token_groups, token_rows, unit_cols)
    weight_split = weight.reshape(feature_groups, weight.shape[0] // feature_groups, unit_cols)
    terms = jnp.einsum(
        "atc,bkc->abtk", grad_split, weight_split, preferred_element_type=jnp.float32
    )
    terms = terms.reshape(token_groups * feature_groups * token_rows, weight_split.shape[1])
    grad_in = lax.psum_scatter(terms, ("gx", "gz"), scatter_dimension=0, tiled=True)
    return (grad_in.astype(jnp.bfloat16), grad_weight)


def solution(mesh):
    return jax.shard_map(
        body,
        mesh=mesh,
        in_specs=(P("gx", ("gy", "gz")), P("gx", ("gz", "gy")), P("gy", ("gz", "gx"))),
        out_specs=(P("gx", ("gy", "gz")), P("gy", ("gz", "gx"))),
        check_vma=False,
    )
```

profile of v0, /device:TPU:0, one launch (start us, length us, event | category | flops | bytes accessed | tf_op | source)
XLA Modules:
  0.0 386.5 jit_solution(9099532467425328987)
XLA Ops:
  7.2 0.0 all-gather.6.cloned.1.call-start
  7.2 0.7 all-gather.6.cloned.1.call-update
  7.9 0.0 all-gather.4.cloned.1.call-start
  7.9 2.0 copy.5
  9.9 0.0 all-gather.4.cloned.1.call-update
  10.0 0.0 all-gather.8.cloned.1.call-start
  10.0 26.1 %all-gather.6.cloned.1.call-done = bf16[128,4096]{1,0:T(8,128)(2,1)} async-done(((bf16[128,1024]{1,0:T(8,128)(2,1)}), bf16[128,4096]{1,0:T(8,128)(2,1)}) %all-gather.6.cloned.1.call-update) | async-done | bytes 1048592 | tf_op jit(solution)/shard_map/all_gather | solution.py:14
  36.1 0.0 all-gather.8.cloned.1.call-update
  36.2 0.0 reduce-scatter.2.cloned.1.call-start
  36.2 27.8 %all-gather.4.cloned.1.call-done = bf16[128,7168]{0,1:T(8,128)(2,1)} async-done(((bf16[128,1792]{0,1:T(8,128)(2,1)}), bf16[128,7168]{0,1:T(8,128)(2,1)}) %all-gather.4.cloned.1.call-update) | async-done | bytes 1835024 | tf_op jit(solution)/shard_map/all_gather | solution.py:11
  64.0 3.1 copy.6
  67.1 46.1 %all_to_all.19 = bf16[128,8,896]{2,0,1:T(8,128)(2,1)S(1)} all-to-all(bf16[128,8,896]{2,0,1:T(8,128)(2,1)S(1)} %copy.6), channel_id=1, replica_groups=mesh['gx'=8,'gy'=4,'gz'=4] {'gx'}, dimensions={1} | all-to-all | bytes 3670016 | tf_op jit(solution)/shard_map/all_to_all | solution.py:12
  113.2 0.0 copy-start
  113.2 11.8 %convolution_bitcast_fusion = f32[8,4,128,1024]{3,2,0,1:T(8,128)S(1)} fusion(bf16[4,1024,896,1]{2,1,3,0:T(8,128)(2,1)} %bitcast.22, bf16[128,8,896]{2,0,1:T(8,128)(2,1)S(1)} %all_to_all.19), kind=kOutput, calls=%fused_computation | convolution fusion | flops 7516192768 | bytes 25952256 | tf_op jit(solution)/shard_map/atc,bkc->abtk/dot_general | solution.py:24
  125.0 0.0 copy-done
  125.0 6.1 %copy.7 = f32[8,4,128,1024]{3,2,1,0:T(8,128)} copy(f32[8,4,128,1024]{3,2,0,1:T(8,128)S(1)} %convolution_bitcast_fusion) | data formatting | bytes 33554432 | tf_op jit(solution)/shard_map/atc,bkc->abtk/transpose | solution.py:24
  131.1 0.0 copy-start.1
  131.1 0.0 reduce-scatter.2.cloned.1.call-update
  131.1 43.9 %all-gather.8.cloned.1.call-done = bf16[1024,4096]{1,0:T(8,128)(2,1)} async-done(((bf16[128,4096]{1,0:T(8,128)(2,1)}), bf16[1024,4096]{1,0:T(8,128)(2,1)}) %all-gather.8.cloned.1.call-update) | async-done | bytes 8388624 | tf_op jit(solution)/shard_map/all_gather | solution.py:17
  175.0 0.0 copy-done.1
  175.1 14.2 %convolution_convert_fusion = bf16[4096,896]{1,0:T(8,128)(2,1)} fusion(bf16[1024,4096]{1,0:T(8,128)(2,1)} %all-gather.8.cloned.1.call-done, bf16[1024,896]{1,0:T(8,128)(2,1)S(1)} %bitcast.21), kind=kOutput, calls=%fused_computation.1 | convolution fusion | flops 7519862784 | bytes 17563648 | tf_op jit(solution)/shard_map/td,tc->dc/dot_general | solution.py:15
  189.3 189.0 %reduce-scatter.2.cloned.1.call-done = f32[128,1024]{1,0:T(8,128)} async-done(((f32[4096,1024]{1,0:T(8,128)}), f32[128,1024]{1,0:T(8,128)}) %reduce-scatter.2.cloned.1.call-update) | async-done | bytes 524304 | tf_op jit(solution)/shard_map/reduce_scatter | solution.py:28
  378.2 1.8 convert_element_type.6
Async XLA Ops:
  7.2 29.0 %all-gather.6.cloned.1.call-start = ((), (), s32[]{:S(2)}) async-start(), calls=%async_computation.4 | async-start | bytes 1310720 | tf_op jit(solution)/shard_map/all_gather | solution.py:14
  7.9 56.1 %all-gather.4.cloned.1.call-start = ((), (), s32[]{:S(2)}) async-start(), calls=%async_computation.2 | async-start | bytes 2293760 | tf_op jit(solution)/shard_map/all_gather | solution.py:11
  10.0 165.1 %all-gather.8.cloned.1.call-start = ((), (), s32[]{:S(2)}) async-start(), calls=%async_computation.5 | async-start | bytes 9437184 | tf_op jit(solution)/shard_map/all_gather | solution.py:17
  36.2 342.1 %reduce-scatter.2.cloned.1.call-start = ((), (), s32[]{:S(2)}) async-start(), calls=%async_computation.3 | async-start | bytes 17301504 | tf_op jit(solution)/shard_map/reduce_scatter | solution.py:28
  113.2 11.8 %copy-start = (bf16[128,8,896]{2,0,1:T(8,128)(2,1)}, bf16[128,8,896]{2,0,1:T(8,128)(2,1)S(1)}, u32[]{:S(2)}) copy-start(bf16[128,8,896]{2,0,1:T(8,128)(2,1)S(1)} %all_to_all.19) | copy-start | bytes 5505028
  131.1 43.9 %copy-start.1 = (bf16[128,8,896]{2,0,1:T(8,128)(2,1)S(1)}, bf16[128,8,896]{2,0,1:T(8,128)(2,1)}, u32[]{:S(2)}) copy-start(bf16[128,8,896]{2,0,1:T(8,128)(2,1)} %copy-done) | copy-start | bytes 5505028
Sparse Core Ops, SparseCore 0:
  9.7 26.4 all-gather.5
  38.4 25.6 all-gather.3
  65.7 109.3 all-gather.7
  177.3 200.8 reduce-scatter.1
where the time goes:
time: 387 us
  waiting for transfers between devices  288 us (74%)
  blocking collectives  46.1 us (12%)
  matrix products  26 us (7%)
  between operations  13.8 us (4%)
  local copies, waits for them, and re-layouts  11.2 us (3%)
    reduce_scatter x1, waiting for transfers between devices, body(): lax.psum_scatter(terms, ('gx', 'gz'), scatter_dimension=0, tiled=True)  189 us
    all_to_all x1, blocking collectives, body(): lax.all_to_all(grad_block, 'gx', split_axis=1, concat_axis=0, tiled=True)  46.1 us
    all_gather x1, waiting for transfers between devices, body(): lax.all_gather(inputs_block, 'gx', axis=0, tiled=True)  43.9 us
    all_gather x1, waiting for transfers between devices, body(): grad_block = lax.all_gather(grad_out, 'gy', axis=1, tiled=True)  27.8 us
    all_gather x1, waiting for transfers between devices, body(): inputs_block = lax.all_gather(x_saved, 'gz', axis=1, tiled=True)  26.1 us
    dot_general x1, matrix products, body(): jnp.einsum('td,tc->dc', lax.all_gather(inputs_block, 'gx', axis=0, tiled=...  14.2 us
    dot_general x1, matrix products, body(): jnp.einsum('atc,bkc->abtk', grad_split, weight_split, preferred_element_t...  11.8 us
  transfers between devices with their start and end apart: 4, of which 4 were waited for; matrix products, arithmetic and copies ran while one was open for 10% of the time, Pallas kernels for 0%

commit v1 on v0

--- a/solution.py
+++ b/solution.py
@@ -11,7 +11,9 @@
     grad_block = lax.all_gather(grad_out, "gy", axis=1, tiled=True)
     grad_all = lax.all_to_all(grad_block, "gx", split_axis=1, concat_axis=0, tiled=True)
     unit_cols = grad_all.shape[1]
-    inputs_block = lax.all_gather(x_saved, "gz", axis=1, tiled=True)
+    inputs_block = jnp.concatenate(
+        lax.all_to_all(jnp.stack([x_saved] * lax.axis_size("gz")), "gz", 0, 0), axis=1
+    )
     summed = jnp.einsum(
         "td,tc->dc",
         lax.all_gather(inputs_block, "gx", axis=0, tiled=True),

time: 387 us -> 372 us (0.961)
  waiting for transfers between devices: 288 us -> 258 us
  blocking collectives: 46.1 us -> 59 us
    all_gather x1 -> x0, waiting for transfers between devices: 26.1 us -> none  [body(): inputs_block = lax.all_gather(x_saved, 'gz', axis=1, tiled=True)]
    all_gather x1, waiting for transfers between devices: 27.8 us -> 7.88 us  [body(): grad_block = lax.all_gather(grad_out, 'gy', axis=1, tiled=True)]
    all_to_all x0 -> x1, blocking collectives: none -> 19.5 us  [body(): lax.all_to_all(jnp.stack([x_saved] * lax.axis_size('gz')), 'gz', 0, 0)]
    all_gather x1, waiting for transfers between devices: 43.9 us -> 58.1 us  [body(): lax.all_gather(inputs_block, 'gx', axis=0, tiled=True)]
    all_to_all x1, blocking collectives: 46.1 us -> 39.5 us  [body(): lax.all_to_all(grad_block, 'gx', split_axis=1, concat_axis=0, tiled=True)]
  transfers between devices with their start and end apart: 4 -> 3, of which waited for: 4 -> 3; matrix products, arithmetic and copies ran while one was open for 10% -> 10% of each run, Pallas kernels for 0% -> 0%
where the time goes in v1:
time: 372 us; the launch traced here: 371 us
  waiting for transfers between devices  258 us (69%)
  blocking collectives  59 us (16%)
  matrix products  26 us (7%)
  between operations  13.8 us (4%)
  local copies, waits for them, and re-layouts  12.5 us (3%)
    reduce_scatter x1, waiting for transfers between devices, body(): lax.psum_scatter(terms, ('gx', 'gz'), scatter_dimension=0, tiled=True)  192 us
    all_gather x1, waiting for transfers between devices, body(): lax.all_gather(inputs_block, 'gx', axis=0, tiled=True)  58.1 us
    all_to_all x1, blocking collectives, body(): lax.all_to_all(grad_block, 'gx', split_axis=1, concat_axis=0, tiled=True)  39.5 us
    all_to_all x1, blocking collectives, body(): lax.all_to_all(jnp.stack([x_saved] * lax.axis_size('gz')), 'gz', 0, 0)  19.5 us
    dot_general x1, matrix products, body(): jnp.einsum('td,tc->dc', lax.all_gather(inputs_block, 'gx', axis=0, tiled=...  14.1 us
    dot_general x1, matrix products, body(): jnp.einsum('atc,bkc->abtk', grad_split, weight_split, preferred_element_t...  11.9 us
    all_gather x1, waiting for transfers between devices, body(): grad_block = lax.all_gather(grad_out, 'gy', axis=1, tiled=True)  7.88 us
  transfers between devices with their start and end apart: 3, of which 3 were waited for; matrix products, arithmetic and copies ran while one was open for 10% of the time, Pallas kernels for 0%

profile of v1, /device:TPU:0, one launch (start us, length us, event | category | flops | bytes accessed | tf_op | source)
XLA Modules:
  0.0 371.2 jit_solution(13003278977156362469)
XLA Ops:
  7.2 0.0 all-gather.3.cloned.1.call-start
  7.2 2.0 copy.5
  9.2 0.0 all-gather.3.cloned.1.call-update
  9.2 0.0 all-gather.5.cloned.1.call-start
  9.3 1.1 copy.8
  10.4 0.1 stack.2
  10.5 19.5 %all_to_all.24 = bf16[4,128,1024]{1,2,0:T(8,128)(2,1)} all-to-all(bf16[4,128,1024]{1,2,0:T(8,128)(2,1)S(1)} %stack.2), channel_id=1, replica_groups=mesh['gx'=8,'gy'=4,'gz'=4] {'gz'}, dimensions={0} | all-to-all | bytes 2097152 | tf_op jit(solution)/shard_map/all_to_all | solution.py:15
  30.1 0.0 all-gather.5.cloned.1.call-update
  30.1 0.0 reduce-scatter.2.cloned.1.call-start
  30.2 7.9 %all-gather.3.cloned.1.call-done = bf16[128,7168]{0,1:T(8,128)(2,1)} async-done(((bf16[128,1792]{0,1:T(8,128)(2,1)}), bf16[128,7168]{0,1:T(8,128)(2,1)}) %all-gather.3.cloned.1.call-update) | async-done | bytes 1835024 | tf_op jit(solution)/shard_map/all_gather | solution.py:11
  38.1 3.1 copy.6
  41.1 39.5 %all_to_all.25 = bf16[128,8,896]{2,0,1:T(8,128)(2,1)S(1)} all-to-all(bf16[128,8,896]{2,0,1:T(8,128)(2,1)S(1)} %copy.6), channel_id=1, replica_groups=mesh['gx'=8,'gy'=4,'gz'=4] {'gx'}, dimensions={1} | all-to-all | bytes 3670016 | tf_op jit(solution)/shard_map/all_to_all | solution.py:12
  80.6 0.0 copy-start
  80.6 11.9 %convolution_bitcast_fusion = f32[8,4,128,1024]{3,2,0,1:T(8,128)S(1)} fusion(bf16[4,1024,896,1]{2,1,3,0:T(8,128)(2,1)} %bitcast.26, bf16[128,8,896]{2,0,1:T(8,128)(2,1)S(1)} %all_to_all.25), kind=kOutput, calls=%fused_computation | convolution fusion | flops 7516192768 | bytes 25952256 | tf_op jit(solution)/shard_map/atc,bkc->abtk/dot_general | solution.py:26
  92.5 0.0 copy-done
  92.5 6.2 %copy.7 = f32[8,4,128,1024]{3,2,1,0:T(8,128)} copy(f32[8,4,128,1024]{3,2,0,1:T(8,128)S(1)} %convolution_bitcast_fusion) | data formatting | bytes 33554432 | tf_op jit(solution)/shard_map/atc,bkc->abtk/transpose | solution.py:26
  98.7 0.0 copy-start.1
  98.7 0.0 reduce-scatter.2.cloned.1.call-update
  98.7 58.1 %all-gather.5.cloned.1.call-done = bf16[1024,4096]{0,1:T(8,128)(2,1)} async-done(((bf16[128,4096]{0,1:T(8,128)(2,1)}), bf16[1024,4096]{0,1:T(8,128)(2,1)}) %all-gather.5.cloned.1.call-update) | async-done | bytes 8388624 | tf_op jit(solution)/shard_map/all_gather | solution.py:19
  156.8 0.0 copy-done.1
  156.8 14.1 %convolution_convert_fusion = bf16[4096,896]{1,0:T(8,128)(2,1)} fusion(bf16[1024,4096]{0,1:T(8,128)(2,1)} %all-gather.5.cloned.1.call-done, bf16[1024,896]{1,0:T(8,128)(2,1)S(1)} %bitcast.25), kind=kOutput, calls=%fused_computation.1 | convolution fusion | flops 7519862784 | bytes 17563648 | tf_op jit(solution)/shard_map/td,tc->dc/dot_general | solution.py:17
  170.9 192.0 %reduce-scatter.2.cloned.1.call-done = f32[128,1024]{1,0:T(8,128)} async-done(((f32[4096,1024]{1,0:T(8,128)}), f32[128,1024]{1,0:T(8,128)}) %reduce-scatter.2.cloned.1.call-update) | async-done | bytes 524304 | tf_op jit(solution)/shard_map/reduce_scatter | solution.py:30
  362.9 1.8 convert_element_type.6
Async XLA Ops:
  7.2 30.9 %all-gather.3.cloned.1.call-start = ((), (), s32[]{:S(2)}) async-start(), calls=%async_computation.3 | async-start | bytes 2293760 | tf_op jit(solution)/shard_map/all_gather | solution.py:11
  9.2 147.5 %all-gather.5.cloned.1.call-start = ((), (), s32[]{:S(2)}) async-start(), calls=%async_computation.5 | async-start | bytes 9437184 | tf_op jit(solution)/shard_map/all_gather | solution.py:19
  30.1 332.8 %reduce-scatter.2.cloned.1.call-start = ((), (), s32[]{:S(2)}) async-start(), calls=%async_computation.4 | async-start | bytes 17301504 | tf_op jit(solution)/shard_map/reduce_scatter | solution.py:30
  80.6 11.9 %copy-start = (bf16[128,8,896]{2,0,1:T(8,128)(2,1)}, bf16[128,8,896]{2,0,1:T(8,128)(2,1)S(1)}, u32[]{:S(2)}) copy-start(bf16[128,8,896]{2,0,1:T(8,128)(2,1)S(1)} %all_to_all.25) | copy-start | bytes 5505028
  98.7 58.1 %copy-start.1 = (bf16[128,8,896]{2,0,1:T(8,128)(2,1)S(1)}, bf16[128,8,896]{2,0,1:T(8,128)(2,1)}, u32[]{:S(2)}) copy-start(bf16[128,8,896]{2,0,1:T(8,128)(2,1)} %copy-done) | copy-start | bytes 5505028
Sparse Core Ops, SparseCore 0:
  10.2 27.7 all-gather.2
  39.6 117.1 all-gather.4
  159.2 203.6 reduce-scatter.1
